TPU v7x, 32 devices: a whole 2x2x4 slice. The times are simulated.
32 devices in a mesh: mode: 8 (over y, x, core), orb: 4 (over z).
Axes of the slice: x: 2, y: 2, z: 4, core: 2. Of those that a mesh axis runs over, the one named last changes fastest.
Arguments:
- correlators: float32 [512, 2, 256, 256], P('mode', None, 'orb'), may hold values from -6 to 6
- density: float32 [2, 256, 256], P(None, 'orb'), may hold values from -6 to 6
- bare_hamiltonian: float32 [2, 256, 256], P(None, 'orb'), may hold values from -0.375 to 0.375
- coupling: float32 [512], P('mode'), may hold values from -0.25 to 0.25
- propagator: float32 [512, 512], P('mode'), may hold values from -0.25 to 0.25
Outputs:
- correlators_out: float32 [512, 2, 256, 256], P('mode', None, 'orb')
- density_out: float32 [2, 256, 256], P(None, 'orb')
All inputs are finite; a program needn't handle non-finite values.
Results may differ from a plain program's by a relative error of at most 0.0001.
Values sent between devices are 32-bit elements; how exact they have to be, the bound alone decides.
No kernel may reach another device: no remote copies, remote signals or barrier semaphores. Data moves between devices by JAX's collectives and lax.ppermute only.
A program may use at most 128 MiB of HBM per device.

v0:
```python
import jax
import jax.numpy as jnp
from jax import lax
from jax.sharding import PartitionSpec as P

time_step = 0.1
field_weight = 0.0625


def contract(form, first, second):
    return jnp.einsum(form, first, second, precision=lax.Precision.HIGHEST)


def left_product(matrix, stack):
    real = contract("ij,mjk->mik", matrix[0], stack[:, 0]) - contract(
        "ij,mjk->mik", matrix[1], stack[:, 1]
    )
    imag = contract("ij,mjk->mik", matrix[0], stack[:, 1]) + contract(
        "ij,mjk->mik", matrix[1], stack[:, 0]
    )
    return jnp.stack([real, imag], axis=1)


def right_product(stack, matrix):
    real = contract("mij,jk->mik", stack[:, 0], matrix[0]) - contract(
        "mij,jk->mik", stack[:, 1], matrix[1]
    )
    imag = contract("mij,jk->mik", stack[:, 0], matrix[1]) + contract(
        "mij,jk->mik", stack[:, 1], matrix[0]
    )
    return jnp.stack([real, imag], axis=1)


def advance(stack, commut, weights, dens):
    turned = jnp.stack([commut[:, 1], -commut[:, 0]], axis=1)
    return stack + time_step * turned + time_step * weights[:, None, None, None] * dens[None]


def modes_substep(stacks, dens, hamil, bare_full, weights):
    commut = left_product(hamil, stacks) - right_product(stacks, hamil)
    updated = advance(stacks, commut, weights, dens)
    partial_value = contract("m,mcij->cij", weights, updated)
    collision = lax.psum(partial_value, ("mode", "orb"))
    dens = dens + time_step * collision
    return (updated, dens, bare_full + field_weight * dens)


def to_whole(stacks):
    return lax.all_to_all(stacks, "orb", split_axis=0, concat_axis=2, tiled=True)


def to_split(stacks):
    return lax.all_to_all(stacks, "orb", split_axis=2, concat_axis=0, tiled=True)


def propagate(stacks, propagator):
    local_modes = stacks.shape[0]
    groups = lax.axis_size("mode")
    flat = stacks.reshape(local_modes, groups, -1)
    spread = lax.all_to_all(flat, "mode", split_axis=1, concat_axis=0, tiled=True)
    entries = spread[:, 0, :]
    mixed = contract("mn,nx->mx", lax.all_gather(propagator, "mode", axis=0, tiled=True), entries)
    returned = lax.all_to_all(mixed[:, None, :], "mode", split_axis=0, concat_axis=1, tiled=True)
    return returned.reshape(stacks.shape)


def on_device(correlators, density, bare_hamiltonian, coupling, propagator):
    dens, bare_full = (
        lax.all_gather(density, "orb", axis=1, tiled=True),
        lax.all_gather(bare_hamiltonian, "orb", axis=1, tiled=True),
    )
    hamil = bare_full + field_weight * dens
    owned = correlators.shape[0] // lax.axis_size("orb")
    weights = lax.dynamic_slice_in_dim(coupling, lax.axis_index("orb") * owned, owned, 0)
    whole = to_whole(correlators)
    for turn in range(2):
        whole, dens, hamil = modes_substep(whole, dens, hamil, bare_full, weights)
    stacks = propagate(to_split(whole), propagator)
    whole = to_whole(stacks)
    whole, dens, hamil = modes_substep(whole, dens, hamil, bare_full, weights)
    stacks = to_split(whole)
    row_count = density.shape[1]
    dens_rows = lax.dynamic_slice_in_dim(dens, lax.axis_index("orb") * row_count, row_count, 1)
    return (stacks, dens_rows)


def solution(mesh):
    in_specs = (
        P("mode", None, "orb", None),
        P(None, "orb", None),
        P(None, "orb", None),
        P("mode"),
        P("mode", None),
    )
    out_specs = (P("mode", None, "orb", None), P(None, "orb", None))
    return jax.shard_map(
        on_device, mesh=mesh, in_specs=in_specs, out_specs=out_specs, check_vma=False
    )
```

profile of v0, /device:TPU:0, one launch (start us, length us, event | category | flops | bytes accessed | tf_op | source)
XLA Modules:
  0.0 1640.5 jit_solution(9633585185455088017)
XLA Ops:
  8.0 6.5 all-to-all-start
  14.6 194.0 %all_gather.10 = f32[2,256,256]{2,1,0:T(8,128)S(1)} all-gather(f32[2,64,256]{2,1,0:T(8,128)S(1)} %copy-done.12), channel_id=1, replica_groups=mesh['mode'=8,'orb'=4] {'orb'}, dimensions={1}, use_global_device_ids=true | all-gather | bytes 655360 | tf_op jit(solution)/shard_map/all_gather | solution.py:69
  208.6 15.9 all_gather.9
  224.6 4.1 copy.64
  228.7 3.4 fusion.12
  232.2 3.4 fusion.13
  235.6 3.8 fusion.15
  239.4 4.1 fusion.14
  243.5 3.8 add_bitcast_fusion.4
  247.3 3.4 subtract_bitcast_fusion.4
  250.7 13.2 subtract_bitcast_fusion.5
  263.9 5.2 add_bitcast_fusion.5
  269.1 2.8 maximum_subtract_fusion
  271.9 2.7 fusion.41
  274.6 4.9 fusion.1
  279.5 3.4 copy-done.1
  282.9 7.8 fusion.10
  291.5 130.2 %all-reduce.4.cloned.1.call-done = f32[2,256,256]{2,1,0:T(8,128)} async-done(((f32[2,256,256]{2,1,0:T(8,128)}), f32[2,256,256]{2,1,0:T(8,128)}) %all-reduce.4.cloned.1.call-update) | async-done | bytes 524304 | tf_op jit(solution)/shard_map/psum | solution.py:43
  423.8 6.1 fusion.21
  429.9 3.4 fusion.20
  433.4 4.0 fusion.23
  437.4 4.0 fusion.22
  441.4 4.3 subtract_bitcast_fusion.2
  445.8 5.0 add_bitcast_fusion.2
  450.7 5.5 subtract_bitcast_fusion.3
  456.3 5.4 add_bitcast_fusion.3
  461.7 4.3 maximum_subtract_fusion.1
  466.0 4.3 fusion.40
  470.3 6.9 fusion.3
  477.2 8.3 copy.81
  485.4 186.8 %all_to_all.99 = f32[16,2,256,256]{3,0,1,2:T(8,128)S(1)} all-to-all(f32[16,2,256,256]{3,0,1,2:T(8,128)} %copy.81), channel_id=1, replica_groups=mesh['mode'=8,'orb'=4] {'orb'}, dimensions={2} | all-to-all | bytes 16777216 | tf_op jit(solution)/shard_map/all_to_all | solution.py:53
  672.3 8.3 copy.145
  680.5 9.4 reshape.18
  689.9 11.6 copy.83
  701.5 5.0 all-to-all-start.2
  707.1 56.9 %all-gather.2.cloned.1.call-done = f32[512,512]{1,0:T(8,128)} async-done(((f32[64,512]{1,0:T(8,128)}), f32[512,512]{1,0:T(8,128)}) %all-gather.2.cloned.1.call-update) | async-done | bytes 1048592 | tf_op jit(solution)/shard_map/all_gather | solution.py:62
  764.0 40.7 %all-to-all-done.2 = f32[64,8,4096]{2,0,1:T(8,128)} async-done(((f32[64,8,4096]{2,0,1:T(8,128)}), f32[64,8,4096]{2,0,1:T(8,128)}, u32[]{:S(2)}, u32[]{:S(2)}) %all-to-all-start.2) | async-done | bytes 8388640 | tf_op jit(solution)/shard_map/all_to_all | solution.py:60
  804.7 30.3 %convolution_bitcast_fusion = f32[512,1,4096]{0,2,1:T(8,128)} fusion(f32[512,4096]{1,0:T(8,128)} %bitcast.41, f32[512,512]{1,0:T(8,128)} %all-gather.2.cloned.1.call-done), kind=kOutput, calls=%fused_computation.19 | convolution fusion | flops 12884901888 | bytes 17825792 | tf_op jit(solution)/shard_map/mn,nx->mx/dot_general | solution.py:11
  835.0 19.3 %copy.84 = f32[512,1,4096]{2,1,0:T(1,128)} copy(f32[512,1,4096]{0,2,1:T(8,128)} %convolution_bitcast_fusion) | data formatting | bytes 16777216 | tf_op jit(solution)/shard_map/broadcast_in_dim | solution.py:63
  854.3 97.8 %all_to_all.100 = f32[512,1,4096]{2,1,0:T(1,128)S(1)} all-to-all(f32[512,1,4096]{2,1,0:T(1,128)} %copy.84), channel_id=1, replica_groups=mesh['mode'=8,'orb'=4] {'mode'}, dimensions={0} | all-to-all | bytes 16777216 | tf_op jit(solution)/shard_map/all_to_all | solution.py:63
  952.1 8.1 copy.134
  960.2 8.5 copy.85
  968.6 9.4 reshape.19
  978.0 5.7 all-to-all-start.4
  983.8 12.9 fusion.8
  997.5 272.8 %all-reduce.6.cloned.1.call-done = f32[2,256,256]{2,1,0:T(8,128)} async-done(((f32[2,256,256]{2,1,0:T(8,128)}), f32[2,256,256]{2,1,0:T(8,128)}) %all-reduce.6.cloned.1.call-update) | async-done | bytes 524304 | tf_op jit(solution)/shard_map/psum | solution.py:43
  1271.5 4.0 copy.86
  1275.5 3.4 fusion.29
  1279.0 3.4 fusion.28
  1282.4 4.2 fusion.31
  1286.6 4.0 fusion.30
  1290.7 3.6 subtract_bitcast_fusion
  1294.3 3.4 add_bitcast_fusion
  1297.7 4.3 subtract_bitcast_fusion.1
  1302.0 5.5 add_bitcast_fusion.1
  1307.5 2.8 maximum_subtract_fusion.2
  1310.3 2.7 fusion.39
  1313.0 3.4 fusion.5
  1316.4 3.2 copy-done.4
  1319.6 8.3 copy.95
  1327.9 5.6 all-to-all-start.5
  1333.6 12.7 fusion.6
  1347.1 272.6 %all-reduce.8.cloned.1.call-done = f32[2,256,256]{2,1,0:T(8,128)} async-done(((f32[2,256,256]{2,1,0:T(8,128)}), f32[2,256,256]{2,1,0:T(8,128)}) %all-reduce.8.cloned.1.call-update) | async-done | bytes 524304 | tf_op jit(solution)/shard_map/psum | solution.py:43
  1621.3 11.6 copy.96
  (52 shorter events, 8.2 us)
Async XLA Ops:
  8.0 6.5 copy-start.14
  8.0 6.6 copy-start.12
  8.0 200.5 %copy-start.13 = (f32[2,64,256]{2,1,0:T(8,128)S(1)}, f32[2,64,256]{2,1,0:T(8,128)}, u32[]{:S(2)}) copy-start(f32[2,64,256]{2,1,0:T(8,128)} %param.7) | copy-start | bytes 393220
  8.0 216.6 %all-to-all-start = ((f32[64,2,64,256]{3,2,1,0:T(8,128)}), f32[64,2,64,256]{3,2,1,0:T(8,128)}, u32[]{:S(2)}, u32[]{:S(2)}) async-start(f32[64,2,64,256]{3,2,1,0:T(8,128)} %param.5), calls=%async_computation | async-start | bytes 16777216 | tf_op jit(solution)/shard_map/all_to_all | solution.py:49
  14.5 407.2 %all-reduce.4.cloned.1.call-start = ((), (), s32[]{:S(2)}) async-start(), calls=%async_computation.6 | async-start | bytes 1048576 | tf_op jit(solution)/shard_map/psum | solution.py:43
  208.6 213.2 %copy-start.8 = (f32[2,256,256]{2,1,0:T(8,128)}, f32[2,256,256]{2,1,0:T(8,128)S(1)}, u32[]{:S(2)}) copy-start(f32[2,256,256]{2,1,0:T(8,128)S(1)} %all_gather.10) | copy-start | bytes 1572868
  224.5 197.2 %copy-start.9 = (f32[2,256,256]{2,1,0:T(8,128)}, f32[2,256,256]{2,1,0:T(8,128)S(1)}, u32[]{:S(2)}) copy-start(f32[2,256,256]{2,1,0:T(8,128)S(1)} %all_gather.9) | copy-start | bytes 1572868
  228.7 45.9 %copy-start = (f32[4,16,2,64,256]{4,3,0,1,2:T(8,128)}, f32[4,16,2,64,256]{4,3,0,1,2:T(8,128)S(1)}, u32[]{:S(2)}) copy-start(f32[4,16,2,64,256]{4,3,0,1,2:T(8,128)S(1)} %copy.64) | copy-start | bytes 25165828
  274.6 4.9 copy-start.5
  279.5 3.4 copy-start.1
  421.7 8.2 copy-start.2
  456.3 5.4 copy-start.7
  456.3 14.0 slice-start
  461.7 8.6 slice-start.1
  466.0 4.3 copy-start.6
  477.2 8.3 copy-start.3
  701.5 103.2 %all-to-all-start.2 = ((f32[64,8,4096]{2,0,1:T(8,128)}), f32[64,8,4096]{2,0,1:T(8,128)}, u32[]{:S(2)}, u32[]{:S(2)}) async-start(f32[64,8,4096]{2,0,1:T(8,128)} %copy.83), calls=%async_computation.2 | async-start | bytes 16777216 | tf_op jit(solution)/shard_map/all_to_all | solution.py:60
  706.5 57.5 %all-gather.2.cloned.1.call-start = ((), (), s32[]{:S(2)}) async-start(), calls=%async_computation.7 | async-start | bytes 1179648 | tf_op jit(solution)/shard_map/all_gather | solution.py:62
  978.0 293.5 %all-to-all-start.4 = ((f32[64,2,64,256]{3,2,1,0:T(8,128)}), f32[64,2,64,256]{3,2,1,0:T(8,128)}, u32[]{:S(2)}, u32[]{:S(2)}) async-start(f32[64,2,64,256]{3,2,1,0:T(8,128)} %reshape.19), calls=%async_computation.4 | async-start | bytes 16777216 | tf_op jit(solution)/shard_map/all_to_all | solution.py:49
  983.7 286.7 %copy-start.10 = (f32[2,256,256]{2,1,0:T(8,128)S(1)}, f32[2,256,256]{2,1,0:T(8,128)}, u32[]{:S(2)}) copy-start(f32[2,256,256]{2,1,0:T(8,128)} %copy-done.9) | copy-start | bytes 1572868
  983.7 286.7 %copy-start.11 = (f32[2,256,256]{2,1,0:T(8,128)S(1)}, f32[2,256,256]{2,1,0:T(8,128)}, u32[]{:S(2)}) copy-start(f32[2,256,256]{2,1,0:T(8,128)} %get-tuple-element.5) | copy-start | bytes 1572868
  983.7 286.7 %all-reduce.6.cloned.1.call-start = ((), (), s32[]{:S(2)}) async-start(), calls=%async_computation.8 | async-start | bytes 1048576 | tf_op jit(solution)/shard_map/psum | solution.py:43
  1316.4 3.3 copy-start.4
  1327.9 293.5 %all-to-all-start.5 = ((f32[16,2,256,256]{3,0,1,2:T(8,128)}), f32[16,2,256,256]{3,0,1,2:T(8,128)}, u32[]{:S(2)}, u32[]{:S(2)}) async-start(f32[16,2,256,256]{3,0,1,2:T(8,128)} %copy.95), calls=%async_computation.5 | async-start | bytes 16777216 | tf_op jit(solution)/shard_map/all_to_all | solution.py:53
  1333.5 286.2 %all-reduce.8.cloned.1.call-start = ((), (), s32[]{:S(2)}) async-start(), calls=%async_computation.9 | async-start | bytes 1048576 | tf_op jit(solution)/shard_map/psum | solution.py:43
Sparse Core Ops, SparseCore 0:
  291.7 130.0 all-reduce.3
  997.6 272.6 all-reduce.5
  1347.2 272.4 all-reduce.7
Sparse Core Ops, SparseCore 1:
  708.9 55.1 all-gather.1
where the time goes:
time: 1650 us; the launch traced here: 1640 us
  waiting for transfers between devices  774 us (47%)
  blocking collectives  494 us (30%)
  matrix products  174 us (11%)
  local copies, waits for them, and re-layouts  120 us (7%)
  other arithmetic  39.6 us (2%)
  starting transfers between devices  22.9 us (1%)
    psum x3, waiting for transfers between devices, modes_substep(): collision = lax.psum(partial_value, ('mode', 'orb'))  676 us
    all_gather x1, blocking collectives, on_device(): lax.all_gather(density, 'orb', axis=1, tiled=True)  194 us
    all_to_all x1, blocking collectives, to_split(): lax.all_to_all(stacks, 'orb', split_axis=2, concat_axis=0, tiled=True)  187 us
    dot_general x28, matrix products, contract(): return jnp.einsum(form, first, second, precision=lax.Precision.HIGHEST)  174 us
    all_to_all x1, blocking collectives, propagate(): lax.all_to_all(mixed[:, None, :], 'mode', split_axis=0, concat_axis=1, ti...  97.8 us
    all_gather x1, waiting for transfers between devices, propagate(): lax.all_gather(propagator, 'mode', axis=0, tiled=True)  56.9 us
    all_to_all x1, waiting for transfers between devices, propagate(): lax.all_to_all(flat, 'mode', split_axis=1, concat_axis=0, tiled=True)  40.7 us
  transfers between devices with their start and end apart: 8, of which 5 were waited for; matrix products, arithmetic and copies ran while one was open for 2% of the time, Pallas kernels for 0%

commit v1 on v0

--- a/solution.py
+++ b/solution.py
@@ -40,7 +40,7 @@
     commut = left_product(hamil, stacks) - right_product(stacks, hamil)
     updated = advance(stacks, commut, weights, dens)
     partial_value = contract("m,mcij->cij", weights, updated)
-    collision = lax.psum(partial_value, ("mode", "orb"))
+    collision = lax.psum(lax.psum(partial_value, "orb"), "mode")
     dens = dens + time_step * collision
     return (updated, dens, bare_full + field_weight * dens)
 

time: 1650 us -> 1470 us (0.89)
  waiting for transfers between devices: 774 us -> 597 us
    psum x3 -> x6, waiting for transfers between devices: 676 us -> 499 us  [modes_substep(): collision = lax.psum(lax.psum(partial_value, 'orb'), 'mode')]
  transfers between devices with their start and end apart: 8 -> 11, of which waited for: 5 -> 8; matrix products, arithmetic and copies ran while one was open for 2% -> 2% of each run, Pallas kernels for 0% -> 0%
where the time goes in v1:
time: 1470 us; the launch traced here: 1460 us
  waiting for transfers between devices  597 us (41%)
  blocking collectives  495 us (34%)
  matrix products  173 us (12%)
  local copies, waits for them, and re-layouts  120 us (8%)
  other arithmetic  39.6 us (3%)
  starting transfers between devices  23.5 us (2%)
  between operations  15 us (1%)
    psum x6, waiting for transfers between devices, modes_substep(): collision = lax.psum(lax.psum(partial_value, 'orb'), 'mode')  499 us
    all_gather x1, blocking collectives, on_device(): lax.all_gather(density, 'orb', axis=1, tiled=True)  194 us
    all_to_all x1, blocking collectives, to_split(): lax.all_to_all(stacks, 'orb', split_axis=2, concat_axis=0, tiled=True)  187 us
    dot_general x28, matrix products, contract(): return jnp.einsum(form, first, second, precision=lax.Precision.HIGHEST)  173 us
    all_to_all x1, blocking collectives, propagate(): lax.all_to_all(mixed[:, None, :], 'mode', split_axis=0, concat_axis=1, ti...  97.8 us
    all_gather x1, waiting for transfers between devices, propagate(): lax.all_gather(propagator, 'mode', axis=0, tiled=True)  56.8 us
    all_to_all x1, waiting for transfers between devices, propagate(): lax.all_to_all(flat, 'mode', split_axis=1, concat_axis=0, tiled=True)  40.7 us
  transfers between devices with their start and end apart: 11, of which 8 were waited for; matrix products, arithmetic and copies ran while one was open for 2% of the time, Pallas kernels for 0%

profile of v1, /device:TPU:0, one launch (start us, length us, event | category | flops | bytes accessed | tf_op | source)
XLA Modules:
  0.0 1463.0 jit_solution(11224714549505785684)
XLA Ops:
  7.2 6.5 all-to-all-start
  13.8 194.0 %all_gather.10 = f32[2,256,256]{2,1,0:T(8,128)S(1)} all-gather(f32[2,64,256]{2,1,0:T(8,128)S(1)} %copy-done.12), channel_id=1, replica_groups=mesh['mode'=8,'orb'=4] {'orb'}, dimensions={1}, use_global_device_ids=true | all-gather | bytes 655360 | tf_op jit(solution)/shard_map/all_gather | solution.py:69
  207.7 15.9 %all_gather.9 = f32[2,256,256]{2,1,0:T(8,128)S(1)} all-gather(f32[2,64,256]{2,1,0:T(8,128)S(1)} %copy-done.13), channel_id=1, replica_groups=mesh['mode'=8,'orb'=4] {'orb'}, dimensions={1}, use_global_device_ids=true | all-gather | bytes 655360 | tf_op jit(solution)/shard_map/all_gather | solution.py:70
  223.8 4.1 copy.64
  227.9 3.4 fusion.12
  231.3 3.4 fusion.13
  234.8 3.8 fusion.15
  238.6 4.1 fusion.14
  242.7 3.8 add_bitcast_fusion.4
  246.5 3.4 subtract_bitcast_fusion.4
  249.9 13.2 subtract_bitcast_fusion.5
  263.1 5.2 add_bitcast_fusion.5
  268.3 2.8 maximum_subtract_fusion
  273.8 4.9 fusion.1
  278.7 3.4 copy-done.1
  282.1 7.8 fusion.10
  290.8 39.6 %all-reduce.7.cloned.1.call-done = f32[2,256,256]{2,1,0:T(8,128)} async-done(((f32[2,256,256]{2,1,0:T(8,128)}), f32[2,256,256]{2,1,0:T(8,128)}) %all-reduce.7.cloned.1.call-update) | async-done | bytes 524304 | tf_op jit(solution)/shard_map/psum | solution.py:43
  330.5 57.7 %all-reduce.9.cloned.1.call-done = f32[2,256,256]{2,1,0:T(8,128)} async-done(((f32[2,256,256]{2,1,0:T(8,128)}), f32[2,256,256]{2,1,0:T(8,128)}) %all-reduce.9.cloned.1.call-update) | async-done | bytes 524304 | tf_op jit(solution)/shard_map/psum | solution.py:43
  390.3 6.1 fusion.21
  396.4 3.4 fusion.20
  399.8 4.0 fusion.23
  403.9 4.0 fusion.22
  407.9 4.3 subtract_bitcast_fusion.2
  412.2 5.0 add_bitcast_fusion.2
  417.2 5.5 subtract_bitcast_fusion.3
  422.7 5.4 add_bitcast_fusion.3
  428.2 4.3 maximum_subtract_fusion.1
  432.5 4.3 fusion.40
  436.8 6.9 fusion.3
  443.7 8.3 copy.81
  451.9 187.2 %all_to_all.99 = f32[16,2,256,256]{3,0,1,2:T(8,128)S(1)} all-to-all(f32[16,2,256,256]{3,0,1,2:T(8,128)} %copy.81), channel_id=1, replica_groups=mesh['mode'=8,'orb'=4] {'orb'}, dimensions={2} | all-to-all | bytes 16777216 | tf_op jit(solution)/shard_map/all_to_all | solution.py:53
  639.2 8.3 copy.145
  647.4 9.4 reshape.18
  656.8 11.6 copy.83
  668.4 5.0 all-to-all-start.2
  674.1 56.8 %all-gather.2.cloned.1.call-done = f32[512,512]{1,0:T(8,128)} async-done(((f32[64,512]{1,0:T(8,128)}), f32[512,512]{1,0:T(8,128)}) %all-gather.2.cloned.1.call-update) | async-done | bytes 1048592 | tf_op jit(solution)/shard_map/all_gather | solution.py:62
  731.0 40.7 %all-to-all-done.2 = f32[64,8,4096]{2,0,1:T(8,128)} async-done(((f32[64,8,4096]{2,0,1:T(8,128)}), f32[64,8,4096]{2,0,1:T(8,128)}, u32[]{:S(2)}, u32[]{:S(2)}) %all-to-all-start.2) | async-done | bytes 8388640 | tf_op jit(solution)/shard_map/all_to_all | solution.py:60
  771.6 30.3 %convolution_bitcast_fusion = f32[512,1,4096]{0,2,1:T(8,128)} fusion(f32[512,4096]{1,0:T(8,128)} %bitcast.41, f32[512,512]{1,0:T(8,128)} %all-gather.2.cloned.1.call-done), kind=kOutput, calls=%fused_computation.19 | convolution fusion | flops 12884901888 | bytes 17825792 | tf_op jit(solution)/shard_map/mn,nx->mx/dot_general | solution.py:11
  801.9 19.3 %copy.84 = f32[512,1,4096]{2,1,0:T(1,128)} copy(f32[512,1,4096]{0,2,1:T(8,128)} %convolution_bitcast_fusion) | data formatting | bytes 16777216 | tf_op jit(solution)/shard_map/broadcast_in_dim | solution.py:63
  821.2 97.8 %all_to_all.100 = f32[512,1,4096]{2,1,0:T(1,128)S(1)} all-to-all(f32[512,1,4096]{2,1,0:T(1,128)} %copy.84), channel_id=1, replica_groups=mesh['mode'=8,'orb'=4] {'mode'}, dimensions={0} | all-to-all | bytes 16777216 | tf_op jit(solution)/shard_map/all_to_all | solution.py:63
  919.0 8.1 copy.134
  927.1 8.5 copy.85
  935.5 9.4 reshape.19
  944.9 5.7 all-to-all-start.4
  950.6 12.5 fusion.8
  964.5 75.9 %all-reduce.11.cloned.1.call-done = f32[2,256,256]{2,1,0:T(8,128)} async-done(((f32[2,256,256]{2,1,0:T(8,128)}), f32[2,256,256]{2,1,0:T(8,128)}) %all-reduce.11.cloned.1.call-update) | async-done | bytes 524304 | tf_op jit(solution)/shard_map/psum | solution.py:43
  1040.4 124.8 %all-reduce.13.cloned.1.call-done = f32[2,256,256]{2,1,0:T(8,128)} async-done(((f32[2,256,256]{2,1,0:T(8,128)}), f32[2,256,256]{2,1,0:T(8,128)}) %all-reduce.13.cloned.1.call-update) | async-done | bytes 524304 | tf_op jit(solution)/shard_map/psum | solution.py:43
  1166.3 4.0 copy.86
  1170.3 3.4 fusion.29
  1173.8 3.4 fusion.28
  1177.2 4.0 fusion.31
  1181.2 4.2 fusion.30
  1185.5 3.6 subtract_bitcast_fusion
  1189.0 3.4 add_bitcast_fusion
  1192.5 4.3 subtract_bitcast_fusion.1
  1196.8 5.5 add_bitcast_fusion.1
  1207.8 3.4 fusion.5
  1211.2 3.2 copy-done.4
  1214.4 8.3 copy.95
  1222.7 5.6 all-to-all-start.5
  1228.4 12.7 fusion.6
  1242.0 74.7 %all-reduce.15.cloned.1.call-done = f32[2,256,256]{2,1,0:T(8,128)} async-done(((f32[2,256,256]{2,1,0:T(8,128)}), f32[2,256,256]{2,1,0:T(8,128)}) %all-reduce.15.cloned.1.call-update) | async-done | bytes 524304 | tf_op jit(solution)/shard_map/psum | solution.py:43
  1316.6 125.9 %all-reduce.17.cloned.1.call-done = f32[2,256,256]{2,1,0:T(8,128)} async-done(((f32[2,256,256]{2,1,0:T(8,128)}), f32[2,256,256]{2,1,0:T(8,128)}) %all-reduce.17.cloned.1.call-update) | async-done | bytes 524304 | tf_op jit(solution)/shard_map/psum | solution.py:43
  1444.1 11.6 copy.96
  (61 shorter events, 17.1 us)
Async XLA Ops:
  7.2 6.5 copy-start.14
  7.2 6.6 copy-start.12
  7.2 200.5 %copy-start.13 = (f32[2,64,256]{2,1,0:T(8,128)S(1)}, f32[2,64,256]{2,1,0:T(8,128)}, u32[]{:S(2)}) copy-start(f32[2,64,256]{2,1,0:T(8,128)} %param.7) | copy-start | bytes 393220
  7.2 216.6 %all-to-all-start = ((f32[64,2,64,256]{3,2,1,0:T(8,128)}), f32[64,2,64,256]{3,2,1,0:T(8,128)}, u32[]{:S(2)}, u32[]{:S(2)}) async-start(f32[64,2,64,256]{3,2,1,0:T(8,128)} %param.5), calls=%async_computation | async-start | bytes 16777216 | tf_op jit(solution)/shard_map/all_to_all | solution.py:49
  13.7 316.8 %all-reduce.7.cloned.1.call-start = ((), (), s32[]{:S(2)}) async-start(), calls=%async_computation.6 | async-start | bytes 1048576 | tf_op jit(solution)/shard_map/psum | solution.py:43
  207.7 180.5 %copy-start.8 = (f32[2,256,256]{2,1,0:T(8,128)}, f32[2,256,256]{2,1,0:T(8,128)S(1)}, u32[]{:S(2)}) copy-start(f32[2,256,256]{2,1,0:T(8,128)S(1)} %all_gather.10) | copy-start | bytes 1572868
  223.7 164.5 %copy-start.9 = (f32[2,256,256]{2,1,0:T(8,128)}, f32[2,256,256]{2,1,0:T(8,128)S(1)}, u32[]{:S(2)}) copy-start(f32[2,256,256]{2,1,0:T(8,128)S(1)} %all_gather.9) | copy-start | bytes 1572868
  227.9 45.9 %copy-start = (f32[4,16,2,64,256]{4,3,0,1,2:T(8,128)}, f32[4,16,2,64,256]{4,3,0,1,2:T(8,128)S(1)}, u32[]{:S(2)}) copy-start(f32[4,16,2,64,256]{4,3,0,1,2:T(8,128)S(1)} %copy.64) | copy-start | bytes 25165828
  273.8 4.9 copy-start.5
  278.7 3.4 copy-start.1
  290.8 97.4 %all-reduce.9.cloned.1.call-start = ((), (), s32[]{:S(2)}) async-start(), calls=%async_computation.7 | async-start | bytes 1048576 | tf_op jit(solution)/shard_map/psum | solution.py:43
  388.2 8.2 copy-start.2
  422.7 5.4 copy-start.7
  422.7 14.0 slice-start
  428.2 8.6 slice-start.1
  432.5 4.3 copy-start.6
  443.6 8.3 copy-start.3
  668.4 103.2 %all-to-all-start.2 = ((f32[64,8,4096]{2,0,1:T(8,128)}), f32[64,8,4096]{2,0,1:T(8,128)}, u32[]{:S(2)}, u32[]{:S(2)}) async-start(f32[64,8,4096]{2,0,1:T(8,128)} %copy.83), calls=%async_computation.2 | async-start | bytes 16777216 | tf_op jit(solution)/shard_map/all_to_all | solution.py:60
  673.4 57.6 %all-gather.2.cloned.1.call-start = ((), (), s32[]{:S(2)}) async-start(), calls=%async_computation.8 | async-start | bytes 1179648 | tf_op jit(solution)/shard_map/all_gather | solution.py:62
  944.9 221.4 %all-to-all-start.4 = ((f32[64,2,64,256]{3,2,1,0:T(8,128)}), f32[64,2,64,256]{3,2,1,0:T(8,128)}, u32[]{:S(2)}, u32[]{:S(2)}) async-start(f32[64,2,64,256]{3,2,1,0:T(8,128)} %reshape.19), calls=%async_computation.4 | async-start | bytes 16777216 | tf_op jit(solution)/shard_map/all_to_all | solution.py:49
  950.6 214.6 %copy-start.10 = (f32[2,256,256]{2,1,0:T(8,128)S(1)}, f32[2,256,256]{2,1,0:T(8,128)}, u32[]{:S(2)}) copy-start(f32[2,256,256]{2,1,0:T(8,128)} %copy-done.9) | copy-start | bytes 1572868
  950.6 214.6 %copy-start.11 = (f32[2,256,256]{2,1,0:T(8,128)S(1)}, f32[2,256,256]{2,1,0:T(8,128)}, u32[]{:S(2)}) copy-start(f32[2,256,256]{2,1,0:T(8,128)} %get-tuple-element.5) | copy-start | bytes 1572868
  950.6 89.8 %all-reduce.11.cloned.1.call-start = ((), (), s32[]{:S(2)}) async-start(), calls=%async_computation.9 | async-start | bytes 1048576 | tf_op jit(solution)/shard_map/psum | solution.py:43
  964.0 201.1 %all-reduce.13.cloned.1.call-start = ((), (), s32[]{:S(2)}) async-start(), calls=%async_computation.10 | async-start | bytes 1048576 | tf_op jit(solution)/shard_map/psum | solution.py:43
  1211.2 3.3 copy-start.4
  1222.7 221.4 %all-to-all-start.5 = ((f32[16,2,256,256]{3,0,1,2:T(8,128)}), f32[16,2,256,256]{3,0,1,2:T(8,128)}, u32[]{:S(2)}, u32[]{:S(2)}) async-start(f32[16,2,256,256]{3,0,1,2:T(8,128)} %copy.95), calls=%async_computation.5 | async-start | bytes 16777216 | tf_op jit(solution)/shard_map/all_to_all | solution.py:53
  1228.3 88.3 %all-reduce.15.cloned.1.call-start = ((), (), s32[]{:S(2)}) async-start(), calls=%async_computation.11 | async-start | bytes 1048576 | tf_op jit(solution)/shard_map/psum | solution.py:43
  1241.9 200.6 %all-reduce.17.cloned.1.call-start = ((), (), s32[]{:S(2)}) async-start(), calls=%async_computation.12 | async-start | bytes 1048576 | tf_op jit(solution)/shard_map/psum | solution.py:43
Sparse Core Ops, SparseCore 0:
  290.9 39.5 all-reduce.6
  333.5 54.6 all-reduce.8
  676.1 54.8 all-gather.1
  964.1 76.1 all-reduce.10
  1043.3 121.7 all-reduce.12
  1242.0 74.5 all-reduce.14
  1319.7 122.7 all-reduce.16
